TPU v7x, 32 devices: a whole 2x2x4 slice. The times are simulated.
32 devices in a mesh: rep: 4 (over y, x), fsdp: 4 (over z), tp: 2 (over core).
Axes of the slice: x: 2, y: 2, z: 4, core: 2. Of those that a mesh axis runs over, the one named last changes fastest.
Arguments:
- tokens: bfloat16 [4096, 8192], P(('rep', 'fsdp'), 'tp'), may hold values from -6 to 6
- cotangent: bfloat16 [4096, 512], P(('rep', 'fsdp'), 'tp'), may hold values from -6 to 6
- weight: bfloat16 [512, 8192], P('fsdp', 'tp'), may hold values from -0.0625 to 0.0625
- momentum: bfloat16 [4, 512, 8192], P('rep', 'fsdp', 'tp'), may hold values from -6 to 6
Outputs:
- projected: bfloat16 [4096, 512], P(('rep', 'fsdp'))
- update: float32 [512, 8192], P('fsdp', 'tp')
- momentum_out: float32 [4, 512, 8192], P('rep', 'fsdp', 'tp')
All inputs are finite; a program needn't handle non-finite values.
Results may differ from a plain program's by a relative error of at most 0.006.
Values may be sent and summed in bfloat16 or wider, within the bound.
A program may use at most 64 MiB of HBM per device.

v0:
```python
import functools
import math

import jax
import jax.numpy as jnp
from jax import lax
from jax.experimental import pallas as pl
from jax.experimental.pallas import tpu as pltpu
from jax.sharding import PartitionSpec as P

BETA_ONE = 0.9
BETA_TWO = 0.99
SOFT_WIDTH = 0.25
LANES = 128
LAG = 4
MESH = pl.DeviceIdType.MESH
F32 = jnp.float32
BF16 = jnp.bfloat16


def step(dims, scale, tok, cot, wgt, mom, proj, upd, grad, *scratch):
    (n, nrep, ntp, pieces, rows, width, share) = dims
    (right_buf, left_buf, part, weights, cots, halves, signs, votes, tally, edge_toks, edge_cots, cots_t) = scratch[:12]
    (rs_s, rs_r, ls_s, ls_r, wrs, wrr, wls, wlr, wps, wpr, vs, vr, ts, tr, cs, cr, hs, hr, es, er) = scratch[12:]
    z, me, t = lax.axis_index("fsdp"), lax.axis_index("rep"), lax.axis_index("tp")
    quarter = weights.shape[1] // nrep
    tp_cols = cot.shape[1]

    def to(axis, at):
        return dict(device_id={axis: at}, device_id_type=MESH)

    def other(off, size, at):
        return lax.rem(at + off, size)

    barrier = pltpu.get_barrier_semaphore()
    for axis, at, size in (("tp", t, ntp), ("rep", me, nrep)):
        for off in range(1, size):
            pl.semaphore_signal(barrier, inc=1, **to(axis, other(off, size, at)))
    for off in (1, n - 1):
        pl.semaphore_signal(barrier, inc=1, **to("fsdp", other(off, n, z)))
    pl.semaphore_wait(barrier, ntp + nrep)

    def cot_copy(off):
        return pltpu.make_async_remote_copy(
            cot, cots.at[t], cs.at[off], cr.at[off], **to("tp", other(off, ntp, t)))

    def half_copy(off):
        return pltpu.make_async_remote_copy(
            halves.at[t], halves.at[t], hs.at[off], hr.at[off], **to("tp", other(off, ntp, t)))

    def weight_slot(shard, rep):
        return weights.at[pl.ds(pl.multiple_of(shard * rows, rows), rows),
                          pl.ds(pl.multiple_of(rep * quarter, LANES), quarter)]

    def weight_line(own, shard, send, recv, target):
        slot = weight_slot(shard, me)
        source = wgt.at[:, pl.ds(pl.multiple_of(me * quarter, LANES), quarter)] if own else slot
        return pltpu.make_async_remote_copy(
            source, slot, send.at[shard], recv.at[shard], **to("fsdp", target))

    def weight_plane(shard, off):
        slot = weight_slot(shard, me)
        return pltpu.make_async_remote_copy(
            slot, slot, wps.at[shard, off], wpr.at[shard, off], **to("rep", other(off, nrep, me)))

    def sum_copy(buf, p, k, send, recv, target):
        slot = buf.at[p, pl.ds(pl.multiple_of(k * rows, rows), rows), :]
        return pltpu.make_async_remote_copy(slot, slot, send.at[p, k], recv.at[p, k], **to("fsdp", target))

    def edge_cot_copy(side, target):
        return pltpu.make_async_remote_copy(
            cots, edge_cots.at[side], es.at[side, pieces], er.at[side, pieces], **to("fsdp", target))

    def edge_tok_copy(side, p, target):
        at = pl.ds(pl.multiple_of(p * width, LANES), width)
        return pltpu.make_async_remote_copy(
            tok.at[:, at], edge_toks.at[side, p], es.at[side, p], er.at[side, p], **to("fsdp", target))

    def vote_copy(p, off):
        return pltpu.make_async_remote_copy(
            signs.at[p, other(off, nrep, me)], votes.at[p, me], vs.at[p, off], vr.at[p, off],
            **to("rep", other(off, nrep, me)))

    def tally_copy(p, off):
        return pltpu.make_async_remote_copy(
            tally.at[p, me], tally.at[p, me], ts.at[p, off], tr.at[p, off],
            **to("rep", other(off, nrep, me)))

    def weight_step(i, first=False):
        for send, recv, shard, target, ok in (
            (wrs, wrr, z - i, z + 1, z + 1 < n), (wls, wlr, z + i, z - 1, z > 0)):
            here = (shard >= 0) & (shard < n)
            if not first:
                @pl.when(here)
                def _():
                    weight_line(False, shard, send, recv, z).wait_recv()
            @pl.when(here & ok)
            def _():
                weight_line(first, shard, send, recv, target).start()
            if not first:
                @pl.when(here)
                def _():
                    for off in range(1, nrep):
                        weight_plane(shard, off).start()

    def turn(source, slot):
        for b in range(ntp):
            cots_t[slot, b * tp_cols:(b + 1) * tp_cols, :] = source[b].T

    def sum_step(tau):
        for side, buf, send, recv, depth, toward in (
            (0, right_buf, rs_s, rs_r, z, z + 1), (1, left_buf, ls_s, ls_r, n - 1 - z, z - 1)):
            i = tau - LAG * depth
            p, j = i // (n - 1), lax.rem(jnp.maximum(i, 0), n - 1)
            k = j if side else n - 1 - j
            inside = (i >= 0) & (i < pieces * (n - 1))
            ahead = (k < z) if side else (k > z)
            @pl.when(inside & (depth == 1) & (j == 0))
            def _():
                @pl.when(p == 0)
                def _():
                    edge_cot_copy(side, z).wait_recv()
                    turn(edge_cots.at[side], side)
                edge_tok_copy(side, p, z).wait_recv()
                buf[p] = jnp.dot(cots_t[side], edge_toks[side, p], preferred_element_type=F32).astype(BF16)
            @pl.when(inside & (ahead | (k == z)) & (depth > 1))
            def _():
                sum_copy(buf, p, k, send, recv, z).wait_recv()
            rk = pl.ds(pl.multiple_of(k * rows, rows), rows)
            @pl.when(inside & ahead & (depth > 0))
            def _():
                buf[p, rk, :] = (buf[p, rk, :].astype(F32) + part[p, rk, :].astype(F32)).astype(BF16)
                sum_copy(buf, p, k, send, recv, toward).start()

    own_rows = pl.ds(pl.multiple_of(z * rows, rows), rows)

    def vote(p):
        for s in range(nrep):
            cut = pl.ds(s * share, share)
            at = pl.ds(pl.multiple_of(p * width + s * share, LANES), share)
            g = (part[p, own_rows, cut].astype(F32) + right_buf[p, own_rows, cut].astype(F32)
                 + left_buf[p, own_rows, cut].astype(F32)) * scale
            grad[:, at] = g.astype(BF16)
            blended = BETA_ONE * mom[0, :, at].astype(F32) + (1.0 - BETA_ONE) * g
            signs[p, s] = jnp.clip(blended / SOFT_WIDTH, -1.0, 1.0).astype(BF16)
        for off in range(1, nrep):
            vote_copy(p, off).start()

    def count(p):
        total = signs[p, me].astype(F32)
        for off in range(1, nrep):
            vote_copy(p, off).wait_recv()
            total = total + votes[p, other(nrep - off, nrep, me)].astype(F32)
        tally[p, me] = jnp.clip(total, -1.0, 1.0).astype(BF16)
        for off in range(1, nrep):
            tally_copy(p, off).start()

    def finish(p):
        for off in range(1, nrep):
            tally_copy(p, off).wait_recv()
        for s in range(nrep):
            upd[:, pl.ds(pl.multiple_of(p * width + s * share, LANES), share)] = tally[p, s]

    def project():
        for i in range(n):
            for shard in ((z - i, z + i) if i > 0 else ()):
                @pl.when((shard >= 0) & (shard < n))
                def _():
                    for off in range(1, nrep):
                        weight_plane(shard, off).wait_recv()
        halves[t] = jnp.zeros(halves.shape[1:], F32)
        @pl.loop(0, pieces)
        def _(p):
            at = pl.ds(pl.multiple_of(p * width, LANES), width)
            halves[t] += lax.dot_general(
                tok[:, at], weights[:, at], (((1,), (1,)), ((), ())), preferred_element_type=F32)
        for off in range(1, ntp):
            half_copy(off).start()

    for off in range(1, ntp):
        cot_copy(off).start()
    weight_step(0, True)
    weights[own_rows, :] = wgt[...]
    cots[t] = cot[...]
    for buf, edge in ((right_buf, 0), (left_buf, n - 1)):
        @pl.when(z == edge)
        def _():
            buf[:, edge * rows:(edge + 1) * rows, :] = jnp.zeros((pieces, rows, width), BF16)
    for off in range(1, ntp):
        cot_copy(off).wait_recv()
    for side, edge, target in ((0, 0, z + 1), (1, n - 1, z - 1)):
        @pl.when(z == edge)
        def _():
            edge_cot_copy(side, target).start()
            for p in range(pieces):
                edge_tok_copy(side, p, target).start()

    turn(cots, 2)

    @pl.loop(0, pieces)
    def _(p):
        at = pl.ds(pl.multiple_of(p * width, LANES), width)
        part[p] = jnp.dot(cots_t[2], tok[:, at], preferred_element_type=F32).astype(BF16)

    sum_step(0)

    @pl.loop(1, n)
    def _(tau):
        weight_step(tau)
        sum_step(tau)

    @pl.loop(n, LAG * (n - 1) + 1)
    def _(tau):
        sum_step(tau)

    @pl.loop(1, pieces)
    def _(p):
        vote(p - 1)
        @pl.when(p > 2)
        def _():
            count(p - 3)
        @pl.loop(1, n)
        def _(j):
            sum_step((p + LAG - 1) * (n - 1) + j)

    vote(pieces - 1)
    for p in range(max(0, pieces - 3), pieces - 1):
        count(p)
    project()
    count(pieces - 1)
    for off in range(1, ntp):
        half_copy(off).wait_recv()
    total = halves[0]
    for b in range(1, ntp):
        total = total + halves[b]
    proj[...] = total.astype(BF16)

    @pl.loop(0, pieces)
    def _(p):
        finish(p)

    for off in range(1, ntp):
        cot_copy(off).wait_send()
        half_copy(off).wait_send()

    @pl.loop(0, pieces)
    def _(p):
        for off in range(1, nrep):
            vote_copy(p, off).wait_send()
            tally_copy(p, off).wait_send()
        for k in range(n):
            @pl.when((k > z) & (z > 0))
            def _():
                sum_copy(right_buf, p, k, rs_s, rs_r, z).wait_send()
            @pl.when((k < z) & (z < n - 1))
            def _():
                sum_copy(left_buf, p, k, ls_s, ls_r, z).wait_send()
    for side, edge in ((0, 0), (1, n - 1)):
        @pl.when(z == edge)
        def _():
            edge_cot_copy(side, z).wait_send()
            for p in range(pieces):
                edge_tok_copy(side, p, z).wait_send()
    for shard in range(n):
        @pl.when((shard <= z) & (z + 1 < n))
        def _():
            weight_line(False, shard, wrs, wrr, z).wait_send()
        @pl.when((shard >= z) & (z > 0))
        def _():
            weight_line(False, shard, wls, wlr, z).wait_send()
        @pl.when(shard != z)
        def _():
            for off in range(1, nrep):
                weight_plane(shard, off).wait_send()


def shards(n, nrep, ntp, tokens, cotangent, weight, momentum):
    held, half = tokens.shape
    rows, cols = weight.shape[0], weight.shape[0] * n
    pieces = max(1, min(8, half // (LANES * nrep)))
    width = half // pieces
    share = width // nrep
    scale = 1.0 / math.sqrt(held * n)
    dma = pltpu.SemaphoreType.DMA
    vmem = pl.BlockSpec(memory_space=pltpu.VMEM)
    projected, update, gradient = pl.pallas_call(
        functools.partial(step, (n, nrep, ntp, pieces, rows, width, share), scale),
        out_shape=(
            jax.ShapeDtypeStruct((held, cols), BF16),
            jax.ShapeDtypeStruct((rows, half), BF16),
            jax.ShapeDtypeStruct((rows, half), BF16),
        ),
        in_specs=[vmem] * 4,
        out_specs=(vmem,) * 3,
        scratch_shapes=[
            pltpu.VMEM((pieces, cols, width), BF16),
            pltpu.VMEM((pieces, cols, width), BF16),
            pltpu.VMEM((pieces, cols, width), BF16),
            pltpu.VMEM((cols, half), BF16),
            pltpu.VMEM((ntp,) + cotangent.shape, BF16),
            pltpu.VMEM((ntp, held, cols), F32),
            pltpu.VMEM((pieces, nrep, rows, share), BF16),
            pltpu.VMEM((pieces, nrep, rows, share), BF16),
            pltpu.VMEM((pieces, nrep, rows, share), BF16),
            pltpu.VMEM((2, pieces, held, width), BF16),
            pltpu.VMEM((2, ntp) + cotangent.shape, BF16),
            pltpu.VMEM((3, cols, held), BF16),
        ]
        + [dma((pieces, n))] * 4
        + [dma((n,))] * 4
        + [dma((n, nrep))] * 2
        + [dma((pieces, nrep))] * 4
        + [dma((ntp,))] * 4
        + [dma((2, pieces + 1))] * 2,
        compiler_params=pltpu.CompilerParams(
            collective_id=0, has_side_effects=True, vmem_limit_bytes=60 * 1024 * 1024
        ),
    )(tokens, cotangent, weight, momentum)
    renewed = BETA_TWO * momentum.astype(F32) + (1.0 - BETA_TWO) * gradient.astype(F32)[None]
    return (projected, update.astype(F32), renewed)


def solution(mesh):
    sizes = dict(mesh.shape)
    return jax.shard_map(
        functools.partial(shards, sizes["fsdp"], sizes["rep"], sizes["tp"]),
        mesh=mesh,
        in_specs=(
            P(("rep", "fsdp"), "tp"),
            P(("rep", "fsdp"), "tp"),
            P("fsdp", "tp"),
            P("rep", "fsdp", "tp"),
        ),
        out_specs=(P(("rep", "fsdp"), None), P("fsdp", "tp"), P("rep", "fsdp", "tp")),
        check_vma=False,
    )
```

profile of v0, /device:TPU:0, one launch (start us, length us, event | category | flops | bytes accessed | tf_op | source)
XLA Modules:
  0.0 93.0 jit_solution(16127720344431842672)
XLA Ops:
  0.6 87.0 %shard_map.67 = (bf16[256,512]{1,0:T(8,128)(2,1)}, bf16[128,4096]{1,0:T(8,128)(2,1)}, bf16[128,4096]{1,0:T(8,128)(2,1)}) custom-call(bf16[256,4096]{1,0:T(8,128)(2,1)} %tok.1, bf16[256,256]{1,0:T(8,128)(2,1)} %cot.1, bf16[128,4096]{1,0:T(8,128)(2,1)} %wgt.1, bf16[1,128,4096]{2,1,0:T(8,128)(2,1)} %mom.1), custom_call_target="tpu_custom_call" | custom-call | tf_op jit(solution)/shard_map/pallas_call | solution.py:286
  87.7 0.0 copy-start
  87.7 0.0 copy-start.1
  87.7 2.9 %convert_element_type.9 = f32[128,4096]{1,0:T(8,128)} convert(bf16[128,4096]{1,0:T(8,128)(2,1)} %get-tuple-element.7) | non-fusion elementwise | flops 524288 | bytes 3145728 | tf_op jit(solution)/shard_map/convert_element_type | solution.py:320
  90.6 0.0 copy-done
  90.6 0.0 copy-done.1
  90.6 0.0 copy-start.2
  90.6 1.7 %bitcast_add_fusion = f32[1,128,4096]{2,1,0:T(8,128)} fusion(bf16[128,4096]{1,0:T(8,128)(2,1)S(1)} %copy-done.1, bf16[1,128,4096]{2,1,0:T(8,128)(2,1)S(1)} %copy-done), kind=kLoop, calls=%fused_computation | loop fusion | flops 2621440 | bytes 4194304 | tf_op jit(solution)/shard_map/add | solution.py:319
  92.3 0.0 copy-done.2
  92.3 0.7 copy.8
Async XLA Ops:
  87.7 2.9 %copy-start = (bf16[1,128,4096]{2,1,0:T(8,128)(2,1)S(1)}, bf16[1,128,4096]{2,1,0:T(8,128)(2,1)}, u32[]{:S(2)}) copy-start(bf16[1,128,4096]{2,1,0:T(8,128)(2,1)} %mom.1) | copy-start | bytes 3145732
  87.7 2.9 %copy-start.1 = (bf16[128,4096]{1,0:T(8,128)(2,1)S(1)}, bf16[128,4096]{1,0:T(8,128)(2,1)}, u32[]{:S(2)}) copy-start(bf16[128,4096]{1,0:T(8,128)(2,1)} %get-tuple-element.8) | copy-start | bytes 3145732
  90.6 1.7 %copy-start.2 = (bf16[256,512]{1,0:T(8,128)(2,1)S(1)}, bf16[256,512]{1,0:T(8,128)(2,1)}, u32[]{:S(2)}) copy-start(bf16[256,512]{1,0:T(8,128)(2,1)} %get-tuple-element.12) | copy-start | bytes 786436
where the time goes:
time: 93.1 us; the launch traced here: 93 us
  Pallas kernels  87 us (93%)
  other arithmetic  4.57 us (5%)
    pallas_call x1, Pallas kernels, shards(): pl.pallas_call(functools.partial(step, (n, nrep, ntp, pieces, rows, width...  87 us
    convert_element_type x1, other arithmetic, shards(): return (projected, update.astype(F32), renewed)  2.9 us

commit v1 on v0

v1 whole, which is shorter than its diff:
```python
import functools
import math

import jax
import jax.numpy as jnp
from jax import lax
from jax.experimental import pallas as pl
from jax.experimental.pallas import tpu as pltpu
from jax.sharding import PartitionSpec as P

BETA_ONE = 0.9
BETA_TWO = 0.99
SOFT_WIDTH = 0.25
LANES = 128
WIDTH = 256
LAG = 3
WLAG = 2
PROJ_STEPS = 8
MESH = pl.DeviceIdType.MESH
F32 = jnp.float32
BF16 = jnp.bfloat16


def step(dims, scale, tok, cot, wgt, mom, proj, upd, grad, *scratch):
    (n, nrep, ntp, pieces, width, rows, low, chunks) = dims
    (tok_v, mom_v, part, right_buf, left_buf, weights, cots, edge_cots, cots_t, edge_cots_t, edge_toks,
     halves, edge_out, edge_in, ones, pairs) = scratch[:16]
    (loc, cs, cr, es, er, fs, fr, ks, kr, rs_s, rs_r, ls_s, ls_r, wrs, wrr, wls, wlr, wps, wpr,
     hs, hr, os, orr, vs, vr, ts, tr) = scratch[16:]
    z, me, t = lax.axis_index("fsdp"), lax.axis_index("rep"), lax.axis_index("tp")
    high = nrep // low
    tp_cols = cot.shape[1]
    held = tok.shape[0]
    share = wgt.shape[1] // (nrep * chunks)
    inner = (z > 0) & (z < n - 1)
    beside = (z == 1) | (z == n - 2)
    own_rows = pl.ds(pl.multiple_of(z * rows, rows), rows)

    def to(axis, at):
        return dict(device_id={axis: at}, device_id_type=MESH)

    def cols(p):
        return pl.ds(pl.multiple_of(p * width, LANES), width)

    def cot_copy(off):
        return pltpu.make_async_remote_copy(
            cot, cots.at[t], cs.at[off], cr.at[off], **to("tp", lax.rem(t + off, ntp)))

    def edge_cot(target):
        return pltpu.make_async_remote_copy(cot, edge_cots.at[t], es.at[0], er.at[0], **to("fsdp", target))

    def edge_cot_relay(off):
        return pltpu.make_async_remote_copy(
            edge_cots.at[t], edge_cots.at[t], fs.at[off], fr.at[off], **to("tp", lax.rem(t + off, ntp)))

    def edge_tok(p, target):
        return pltpu.make_async_remote_copy(
            tok.at[:, cols(p)], edge_toks.at[p], ks.at[p], kr.at[p], **to("fsdp", target))

    def sum_copy(buf, p, k, send, recv, target):
        slot = buf.at[p, pl.ds(pl.multiple_of(k * rows, rows), rows), :]
        return pltpu.make_async_remote_copy(slot, slot, send.at[p, k], recv.at[p, k], **to("fsdp", target))

    def weight_cols(c):
        return pl.ds(pl.multiple_of((me * chunks + c) * share, LANES), share)

    def weight_slot(shard, c):
        return weights.at[pl.ds(pl.multiple_of(shard * rows, rows), rows), weight_cols(c)]

    def weight_line(own, shard, c, send, recv, target):
        slot = weight_slot(shard, c)
        source = wgt.at[:, weight_cols(c)] if own else slot
        return pltpu.make_async_remote_copy(
            source, slot, send.at[shard, c], recv.at[shard, c], **to("fsdp", target))

    def weight_plane(shard, c, off):
        slot = weight_slot(shard, c)
        return pltpu.make_async_remote_copy(
            slot, slot, wps.at[shard, c, off], wpr.at[shard, c, off], **to("rep", lax.rem(me + off, nrep)))

    def half_copy(off):
        return pltpu.make_async_remote_copy(
            halves.at[t], halves.at[t], hs.at[off], hr.at[off], **to("tp", lax.rem(t + off, ntp)))

    def out_copy(target):
        return pltpu.make_async_remote_copy(edge_out, edge_in, os.at[0], orr.at[0], **to("fsdp", target))

    def group(stage, p):
        mine, rest = lax.rem(me, low), me // low
        turn = lax.rem(p, 2) if low == high else 0
        along = turn if stage == 0 else 1 - turn
        size = (low, high)[stage]
        at = (1 - along) * mine + along * rest

        def peer(off):
            pos = lax.rem(at + off, size)
            return (1 - along) * (rest * low + pos) + along * (pos * low + mine)

        return size, at, peer

    def vote_copy(stage, p, off):
        _, at, peer = group(stage, p)
        slot = (ones, pairs)[stage].at[p, at]
        send, recv = ((vs, vr), (ts, tr))[stage]
        return pltpu.make_async_remote_copy(slot, slot, send.at[p, off], recv.at[p, off], **to("rep", peer(off)))

    def turned(source, target):
        for b in range(ntp):
            target[b * tp_cols:(b + 1) * tp_cols, :] = source[b].T

    def weight_step(s):
        for h in range(1, n - 1):
            for send, recv, shard, target, edge in (
                (wrs, wrr, z - h, z + 1, z - h == 0), (wls, wlr, z + h, z - 1, z + h == n - 1)):
                c = s - WLAG * (h - 1) - jnp.where(edge, 2, 0)
                on = (target > 0) & (target < n - 1)

                @pl.when(inner & (shard >= 0) & (shard < n) & (c >= 0) & (c < chunks))
                def _():
                    weight_line(False, shard, c, send, recv, z).wait_recv()

                    @pl.when(on)
                    def _():
                        weight_line(False, shard, c, send, recv, target).start()

                    for off in range(1, nrep):
                        weight_plane(shard, c, off).start()

    def token_step(s):
        @pl.when(beside & (s < pieces))
        def _():
            @pl.when(s == 0)
            def _():
                edge_cot(z).wait_recv()
                for off in range(1, ntp):
                    edge_cot_relay(off).start()
                for off in range(1, ntp):
                    edge_cot_relay(off).wait_recv()
                turned(edge_cots, edge_cots_t)

            edge_tok(s, z).wait_recv()
            total = jnp.dot(edge_cots_t[...], edge_toks[s], preferred_element_type=F32) + part[s].astype(F32)

            @pl.when(z == 1)
            def _():
                right_buf[s] = total.astype(BF16)

            @pl.when(z == n - 2)
            def _():
                left_buf[s] = total.astype(BF16)

    flows = ((right_buf, rs_s, rs_r, 1, z), (left_buf, ls_s, ls_r, -1, n - 1 - z))

    def sum_step(s):
        for first in (True, False):
            for j in range(n - 2, 0, -1):
                p = s - LAG * (n - 2 - j)
                for buf, send, recv, way, depth in flows:
                    k = z + way * j
                    ok = (p >= 0) & (p < pieces) & (k >= 0) & (k < n)

                    @pl.when(ok & ((depth == 1) if first else (depth > 1)))
                    def _():
                        if not first:
                            rk = pl.ds(pl.multiple_of(k * rows, rows), rows)
                            sum_copy(buf, p, k, send, recv, z).wait_recv()
                            buf[p, rk, :] = (buf[p, rk, :].astype(F32) + part[p, rk, :].astype(F32)).astype(BF16)
                        sum_copy(buf, p, k, send, recv, z + way).start()

    def vote(p):
        for buf, send, recv, way, depth in flows:
            @pl.when(depth > 1)
            def _():
                sum_copy(buf, p, z, send, recv, z).wait_recv()
        keep = jnp.where(beside, 0.0, 1.0).astype(F32)
        g = (part[p, own_rows, :].astype(F32) * keep + right_buf[p, own_rows, :].astype(F32)
             + left_buf[p, own_rows, :].astype(F32)) * scale
        grad[:, cols(p)] = g.astype(BF16)
        blended = BETA_ONE * mom_v[:, cols(p)].astype(F32) + (1.0 - BETA_ONE) * g
        size, at, _ = group(0, p)
        ones[p, at] = jnp.clip(blended / SOFT_WIDTH, -1.0, 1.0).astype(BF16)
        for off in range(1, size):
            vote_copy(0, p, off).start()

    def added(stage, p):
        size, at, _ = group(stage, p)
        for off in range(1, size):
            vote_copy(stage, p, off).wait_recv()
        buf = (ones, pairs)[stage]
        total = buf[p, 0].astype(F32)
        for i in range(1, size):
            total = total + buf[p, i].astype(F32)
        return total

    def count(p):
        total = added(0, p)
        size, at, _ = group(1, p)
        pairs[p, at] = total.astype(BF16)
        for off in range(1, size):
            vote_copy(1, p, off).start()

    def finish(p):
        upd[:, cols(p)] = jnp.clip(added(1, p), -1.0, 1.0).astype(BF16)
        for stage in range(2):
            for off in range(1, group(stage, p)[0]):
                vote_copy(stage, p, off).wait_send()
        for j in range(1, n - 1):
            for buf, send, recv, way, depth in flows:
                k = z + way * j

                @pl.when((depth > 0) & (k >= 0) & (k < n))
                def _():
                    sum_copy(buf, p, k, send, recv, z).wait_send()

        @pl.when((z == 0) | (z == n - 1))
        def _():
            edge_tok(p, z).wait_send()

    first_proj = 2 + chunks + WLAG * (n - 3) + 3
    per = -(-pieces // PROJ_STEPS)

    def project(s):
        @pl.when(inner & (s == first_proj))
        def _():
            for shard in range(n):
                @pl.when(shard != z)
                def _():
                    @pl.loop(0, chunks)
                    def _(c):
                        for off in range(1, nrep):
                            weight_plane(shard, c, off).wait_recv()
            halves[t] = jnp.zeros(halves.shape[1:], F32)

        @pl.when(inner & (s >= first_proj) & (s < first_proj + PROJ_STEPS))
        def _():
            for i in range(per):
                p = (s - first_proj) * per + i

                @pl.when(p < pieces)
                def _():
                    w = weights[:, cols(p)]
                    halves[t, 0] += lax.dot_general(
                        tok_v[:, cols(p)], w, (((1,), (1,)), ((), ())), preferred_element_type=F32)

                    @pl.when(beside)
                    def _():
                        halves[t, 1] += lax.dot_general(
                            edge_toks[p], w, (((1,), (1,)), ((), ())), preferred_element_type=F32)

        @pl.when(inner & (s == first_proj + PROJ_STEPS))
        def _():
            for off in range(1, ntp):
                half_copy(off).start()

        @pl.when(inner & (s == first_proj + PROJ_STEPS + 1))
        def _():
            for off in range(1, ntp):
                half_copy(off).wait_recv()
            for which, target in ((0, proj), (1, edge_out)):
                total = halves[0, which]
                for b in range(1, ntp):
                    total = total + halves[b, which]
                target[...] = total.astype(BF16)

            @pl.when(z == 1)
            def _():
                out_copy(z - 1).start()

            @pl.when(z == n - 2)
            def _():
                out_copy(z + 1).start()

            for off in range(1, ntp):
                half_copy(off).wait_send()
            for shard in range(n):
                @pl.when(shard != z)
                def _():
                    @pl.loop(0, chunks)
                    def _(c):
                        for off in range(1, nrep):
                            weight_plane(shard, c, off).wait_send()

    tok_load = pltpu.make_async_copy(tok, tok_v, loc.at[0])
    mom_load = pltpu.make_async_copy(mom.at[0], mom_v, loc.at[1])
    cot_load = pltpu.make_async_copy(cot, cots.at[t], loc.at[2])
    wgt_load = pltpu.make_async_copy(wgt, weights.at[own_rows, :], loc.at[3])
    barrier = pltpu.get_barrier_semaphore()
    for axis, at, size in (("tp", t, ntp), ("rep", me, nrep)):
        for off in range(1, size):
            pl.semaphore_signal(barrier, inc=1, **to(axis, lax.rem(at + off, size)))

    @pl.when(z > 0)
    def _():
        pl.semaphore_signal(barrier, inc=1, **to("fsdp", z - 1))

    @pl.when(z < n - 1)
    def _():
        pl.semaphore_signal(barrier, inc=1, **to("fsdp", z + 1))

    cot_load.start()
    tok_load.start()
    wgt_load.start()
    mom_load.start()
    pl.semaphore_wait(barrier, ntp + nrep - 2 + jnp.where(inner, 2, 1))

    for edge, target, send, recv in ((0, z + 1, wrs, wrr), (n - 1, z - 1, wls, wlr)):
        @pl.when(z == edge)
        def _():
            edge_cot(target).start()
            for p in range(2):
                edge_tok(p, target).start()

    for off in range(1, ntp):
        cot_copy(off).start()

    for send, recv, target in ((wrs, wrr, z + 1), (wls, wlr, z - 1)):
        @pl.when(inner & (target > 0) & (target < n - 1))
        def _():
            @pl.loop(0, chunks)
            def _(c):
                weight_line(True, z, c, send, recv, target).start()

    for edge, target, send, recv in ((0, z + 1, wrs, wrr), (n - 1, z - 1, wls, wlr)):
        @pl.when(z == edge)
        def _():
            @pl.loop(2, pieces)
            def _(p):
                @pl.when(p - 2 < chunks)
                def _():
                    weight_line(True, z, p - 2, send, recv, target).start()

                edge_tok(p, target).start()

    for buf, edge in ((right_buf, 0), (left_buf, n - 1)):
        @pl.when(z == edge)
        def _():
            buf[:, edge * rows:(edge + 1) * rows, :] = jnp.zeros((pieces, rows, width), BF16)
    cot_load.wait()
    for off in range(1, ntp):
        cot_copy(off).wait_recv()
    turned(cots, cots_t)
    tok_load.wait()

    @pl.loop(0, pieces)
    def _(p):
        part[p] = jnp.dot(cots_t[...], tok_v[:, cols(p)], preferred_element_type=F32).astype(BF16)

    wgt_load.wait()
    mom_load.wait()

    voting = LAG * (n - 2)
    last = max(pieces + voting + 4, first_proj + PROJ_STEPS + 2)

    @pl.loop(0, last)
    def _(s):
        weight_step(s)
        token_step(s)
        sum_step(s)
        for work, at in ((vote, voting), (count, voting + 2), (finish, voting + 4)):
            @pl.when((s >= at) & (s < at + pieces))
            def _():
                work(s - at)
        project(s)

    for edge, target, send, recv in ((0, z + 1, wrs, wrr), (n - 1, z - 1, wls, wlr)):
        @pl.when(z == edge)
        def _():
            out_copy(target).wait_recv()
            proj[...] = edge_in[...]
            edge_cot(target).wait_send()

            @pl.loop(0, chunks)
            def _(c):
                weight_line(True, z, c, send, recv, target).wait_send()

    for off in range(1, ntp):
        cot_copy(off).wait_send()

    @pl.when(beside)
    def _():
        for off in range(1, ntp):
            edge_cot_relay(off).wait_send()
        out_copy(z).wait_send()

    for shard in range(n):
        for send, recv, target, ok in ((wrs, wrr, z + 1, shard <= z), (wls, wlr, z - 1, shard >= z)):
            @pl.when(inner & ok & (target > 0) & (target < n - 1))
            def _():
                @pl.loop(0, chunks)
                def _(c):
                    weight_line(False, shard, c, send, recv, target).wait_send()


def shards(n, nrep, ntp, tokens, cotangent, weight, momentum):
    held, half = tokens.shape
    rows, cols = weight.shape[0], weight.shape[0] * n
    width = min(WIDTH, half)
    pieces = half // width
    low = max(r for r in range(1, nrep + 1) if nrep % r == 0 and r * r <= nrep)
    chunks = max(1, min(4, half // (nrep * LANES)))
    most = max(low, nrep // low)
    scale = 1.0 / math.sqrt(held * n)
    dma = pltpu.SemaphoreType.DMA
    vmem = pl.BlockSpec(memory_space=pltpu.VMEM)
    hbm = pl.BlockSpec(memory_space=pltpu.HBM)
    projected, update, gradient = pl.pallas_call(
        functools.partial(step, (n, nrep, ntp, pieces, width, rows, low, chunks), scale),
        out_shape=(
            jax.ShapeDtypeStruct((held, cols), BF16),
            jax.ShapeDtypeStruct((rows, half), BF16),
            jax.ShapeDtypeStruct((rows, half), BF16),
        ),
        in_specs=[hbm] * 4,
        out_specs=(vmem,) * 3,
        scratch_shapes=[
            pltpu.VMEM((held, half), BF16),
            pltpu.VMEM((rows, half), BF16),
            pltpu.VMEM((pieces, cols, width), BF16),
            pltpu.VMEM((pieces, cols, width), BF16),
            pltpu.VMEM((pieces, cols, width), BF16),
            pltpu.VMEM((cols, half), BF16),
            pltpu.VMEM((ntp,) + cotangent.shape, BF16),
            pltpu.VMEM((ntp,) + cotangent.shape, BF16),
            pltpu.VMEM((cols, held), BF16),
            pltpu.VMEM((cols, held), BF16),
            pltpu.VMEM((pieces, held, width), BF16),
            pltpu.VMEM((ntp, 2, held, cols), F32),
            pltpu.VMEM((held, cols), BF16),
            pltpu.VMEM((held, cols), BF16),
            pltpu.VMEM((pieces, most, rows, width), BF16),
            pltpu.VMEM((pieces, most, rows, width), BF16),
        ]
        + [dma((4,))]
        + [dma((ntp,))] * 2
        + [dma((1,))] * 2
        + [dma((ntp,))] * 2
        + [dma((pieces,))] * 2
        + [dma((pieces, n))] * 4
        + [dma((n, chunks))] * 4
        + [dma((n, chunks, nrep))] * 2
        + [dma((ntp,))] * 2
        + [dma((1,))] * 2
        + [dma((pieces, most))] * 4,
        compiler_params=pltpu.CompilerParams(
            collective_id=0, has_side_effects=True, vmem_limit_bytes=44 * 1024 * 1024
        ),
    )(tokens, cotangent, weight, momentum)
    renewed = BETA_TWO * momentum.astype(F32) + (1.0 - BETA_TWO) * gradient.astype(F32)[None]
    return (projected, update.astype(F32), renewed)


def solution(mesh):
    sizes = dict(mesh.shape)
    return jax.shard_map(
        functools.partial(shards, sizes["fsdp"], sizes["rep"], sizes["tp"]),
        mesh=mesh,
        in_specs=(
            P(("rep", "fsdp"), "tp"),
            P(("rep", "fsdp"), "tp"),
            P("fsdp", "tp"),
            P("rep", "fsdp", "tp"),
        ),
        out_specs=(P(("rep", "fsdp"), None), P("fsdp", "tp"), P("rep", "fsdp", "tp")),
        check_vma=False,
    )
```

time: 93.1 us -> 95.6 us (1.027)
  local copies, waits for them, and re-layouts: 0.72 us -> 5.64 us
  other arithmetic: 4.57 us -> 3.2 us
  Pallas kernels: 87 us -> 85.9 us
    unnamed x7 -> x9, local copies, waits for them, and re-layouts: 0.72 us -> 5.64 us
    convert_element_type x1, other arithmetic: 2.9 us -> 1.53 us  [shards(): return (projected, update.astype(F32), renewed)]
    pallas_call x1, Pallas kernels: 87 us -> 85.9 us  [shards(): pl.pallas_call(functools.partial(step, (n, nrep, ntp, pieces, width, rows...]
where the time goes in v1:
time: 95.6 us; the launch traced here: 95.4 us
  Pallas kernels  85.9 us (90%)
  local copies, waits for them, and re-layouts  5.64 us (6%)
  other arithmetic  3.2 us (3%)
    pallas_call x1, Pallas kernels, shards(): pl.pallas_call(functools.partial(step, (n, nrep, ntp, pieces, width, rows...  85.9 us
    unnamed x9, local copies, waits for them, and re-layouts  5.64 us

profile of v1, /device:TPU:0, one launch (start us, length us, event | category | flops | bytes accessed | tf_op | source)
XLA Modules:
  0.0 95.4 jit_solution(302362084416697544)
XLA Ops:
  0.6 0.0 copy-start
  0.6 1.2 %copy-done = bf16[1,128,4096]{2,1,0:T(8,128)(2,1)S(1)} copy-done((bf16[1,128,4096]{2,1,0:T(8,128)(2,1)S(1)}, bf16[1,128,4096]{2,1,0:T(8,128)(2,1)}, u32[]{:S(2)}) %copy-start) | copy-done | bytes 1048600
  1.9 0.0 copy-start.1
  1.9 1.6 %copy-done.1 = bf16[256,4096]{1,0:T(8,128)(2,1)S(1)} copy-done((bf16[256,4096]{1,0:T(8,128)(2,1)S(1)}, bf16[256,4096]{1,0:T(8,128)(2,1)}, u32[]{:S(2)}) %copy-start.1) | copy-done | bytes 2097176
  3.4 0.0 copy-start.2
  3.5 1.2 %copy-done.2 = bf16[128,4096]{1,0:T(8,128)(2,1)S(1)} copy-done((bf16[128,4096]{1,0:T(8,128)(2,1)S(1)}, bf16[128,4096]{1,0:T(8,128)(2,1)}, u32[]{:S(2)}) %copy-start.2) | copy-done | bytes 1048600
  4.7 0.0 copy-start.3
  4.7 0.9 copy-done.3
  5.6 85.9 %shard_map.67 = (bf16[256,512]{1,0:T(8,128)(2,1)S(1)}, bf16[128,4096]{1,0:T(8,128)(2,1)S(1)}, bf16[128,4096]{1,0:T(8,128)(2,1)S(1)}) custom-call(bf16[256,4096]{1,0:T(8,128)(2,1)S(1)} %copy-done.1, bf16[256,256]{1,0:T(8,128)(2,1)S(1)} %copy-done.3, bf16[128,4096]{1,0:T(8,128)(2,1)S(1)} %copy-done.2, bf16[1,128,4096]{2,1,0:T(8,128)(2,1)S(1)} %copy-done), custom_call_target="tpu_custom_call" | custom-call | tf_op jit(solution)/shard_map/pallas_call | solution.py:406
  91.4 1.5 %convert_element_type.9 = f32[128,4096]{1,0:T(8,128)} convert(bf16[128,4096]{1,0:T(8,128)(2,1)S(1)} %get-tuple-element.7) | non-fusion elementwise | flops 524288 | bytes 3145728 | tf_op jit(solution)/shard_map/convert_element_type | solution.py:449
  93.0 1.7 %bitcast_add_fusion = f32[1,128,4096]{2,1,0:T(8,128)} fusion(bf16[128,4096]{1,0:T(8,128)(2,1)S(1)} %get-tuple-element.8, bf16[1,128,4096]{2,1,0:T(8,128)(2,1)S(1)} %copy-done), kind=kLoop, calls=%fused_computation | loop fusion | flops 2621440 | bytes 4194304 | tf_op jit(solution)/shard_map/add | solution.py:448
  94.7 0.7 copy.8
Async XLA Ops:
  0.6 1.2 %copy-start = (bf16[1,128,4096]{2,1,0:T(8,128)(2,1)S(1)}, bf16[1,128,4096]{2,1,0:T(8,128)(2,1)}, u32[]{:S(2)}) copy-start(bf16[1,128,4096]{2,1,0:T(8,128)(2,1)} %mom.1) | copy-start | bytes 3145732
  1.9 1.6 %copy-start.1 = (bf16[256,4096]{1,0:T(8,128)(2,1)S(1)}, bf16[256,4096]{1,0:T(8,128)(2,1)}, u32[]{:S(2)}) copy-start(bf16[256,4096]{1,0:T(8,128)(2,1)} %tok.1) | copy-start | bytes 6291460
  3.4 1.2 %copy-start.2 = (bf16[128,4096]{1,0:T(8,128)(2,1)S(1)}, bf16[128,4096]{1,0:T(8,128)(2,1)}, u32[]{:S(2)}) copy-start(bf16[128,4096]{1,0:T(8,128)(2,1)} %wgt.1) | copy-start | bytes 3145732
  4.7 0.9 copy-start.3

commit v2 on v1

v2 whole, which is shorter than its diff:
```python
import functools
import math

import jax
import jax.numpy as jnp
from jax import lax
from jax.experimental import pallas as pl
from jax.experimental.pallas import tpu as pltpu
from jax.sharding import PartitionSpec as P

BETA_ONE = 0.9
BETA_TWO = 0.99
SOFT_WIDTH = 0.25
LANES = 128
WIDTH = 256
LAG = 3
HOLD = 1
BURST = 2
WLAG = 2
RELAY = 3
COUNT = 4
FINISH = 4
PROJ_STEPS = 8
MESH = pl.DeviceIdType.MESH
F32 = jnp.float32
BF16 = jnp.bfloat16


def step(dims, scale, tok, cot, wgt, mom, proj, upd, grad, *scratch):
    (n, nrep, ntp, pieces, width, rows, low, chunks) = dims
    (tok_v, mom_v, part, right_buf, left_buf, weights, cots, edge_cots, cots_t, edge_cots_t, edge_toks,
     halves, edge_half, edge_got, edge_out, edge_in, proj_v, upd_v, grad_v, ones, pairs) = scratch[:21]
    (loc, cs, cr, es, er, fs, fr, ks, kr, rs_s, rs_r, ls_s, ls_r, wrs, wrr, wls, wlr, wps, wpr, wqs,
     hs, hr, gs, gr, os, orr, qs, qr, vs, vr, ts, tr, us, ds) = scratch[21:]
    held_rows = tok.shape[0]
    z, me, t = lax.axis_index("fsdp"), lax.axis_index("rep"), lax.axis_index("tp")
    high = nrep // low
    split = ones.shape[0] // pieces
    part_width = width // split
    band = held_rows // ntp
    tp_cols = cot.shape[1]
    share = wgt.shape[1] // (nrep * chunks)
    inner = (z > 0) & (z < n - 1)
    beside = (z == 1) | (z == n - 2)
    own_rows = pl.ds(pl.multiple_of(z * rows, rows), rows)

    def to(axis, at):
        return dict(device_id={axis: at}, device_id_type=MESH)

    def cols(p):
        return pl.ds(pl.multiple_of(p * width, LANES), width)

    flows = ((right_buf, rs_s, rs_r, 1, z), (left_buf, ls_s, ls_r, -1, n - 1 - z))

    def cot_copy(off):
        return pltpu.make_async_remote_copy(
            cot, cots.at[t], cs.at[off - 1], cr.at[off - 1], **to("tp", lax.rem(t + off, ntp)))

    def edge_cot(target):
        return pltpu.make_async_remote_copy(cot, edge_cots.at[t], es.at[0], er.at[0], **to("fsdp", target))

    def edge_cot_relay(off):
        return pltpu.make_async_remote_copy(
            edge_cots.at[t], edge_cots.at[t], fs.at[off - 1], fr.at[off - 1], **to("tp", lax.rem(t + off, ntp)))

    def edge_tok(p, target):
        return pltpu.make_async_remote_copy(
            tok.at[:, cols(p)], edge_toks.at[p], ks.at[0], kr.at[p], **to("fsdp", target))

    def sum_copy(flow, p, k, sent=True):
        buf, send, recv, way, _ = flow
        slot = buf.at[p, pl.ds(pl.multiple_of(k * rows, rows), rows), :]
        hop = (k - z) * way
        return pltpu.make_async_remote_copy(
            slot, slot, send.at[k], recv.at[p, hop - 1 if sent else hop], **to("fsdp", z + way if sent else z))

    def sums_sent(flow, k):
        buf, send, recv, way, _ = flow
        slot = buf.at[:, pl.ds(pl.multiple_of(k * rows, rows), rows), :]
        return pltpu.make_async_remote_copy(slot, slot, send.at[k], recv.at[0, 0], **to("fsdp", z))

    def weight_cols(c):
        return pl.ds(pl.multiple_of((me * chunks + c) * share, LANES), share)

    def weight_slot(shard, c):
        return weights.at[pl.ds(pl.multiple_of(shard * rows, rows), rows), weight_cols(c)]

    def weight_line(own, shard, c, send, recv, target):
        slot = weight_slot(shard, c)
        source = wgt.at[:, weight_cols(c)] if own else slot
        return pltpu.make_async_remote_copy(
            source, slot, send.at[shard], recv.at[shard, c], **to("fsdp", target))

    def line_sent(shard, send):
        slot = plane_slot(shard, me)
        return pltpu.make_async_remote_copy(slot, slot, send.at[shard], wrr.at[shard, 0], **to("fsdp", z))

    mine, rest = lax.rem(me, low), me // low
    sizes = (low, high)

    def beside_me(way, off):
        if way == 0:
            return rest * low + lax.rem(mine + off, low)
        return lax.rem(rest + off, high) * low + mine

    def before_me(way, off):
        if way == 0:
            return rest * low + lax.rem(mine + low - off, low)
        return lax.rem(rest + high - off, high) * low + mine

    def plane_slot(shard, source, lo=0, hi=None):
        hi = chunks if hi is None else hi
        return weights.at[pl.ds(pl.multiple_of(shard * rows, rows), rows),
                          pl.ds(pl.multiple_of((source * chunks + lo) * share, LANES), (hi - lo) * share)]

    def plane_bytes(count):
        return weights.at[0:(n - 1) * rows, 0:count * share]

    def weight_plane(shard, way, off):
        slot = plane_slot(shard, me)
        return pltpu.make_async_remote_copy(
            slot, slot, wps.at[way, off - 1], wpr.at[shard, me], **to("rep", beside_me(way, off)))

    cut = (chunks + 1) // 2
    cuts = ((0, cut), (cut, chunks))

    def weight_relay(shard, way, off, onward):
        source = before_me(way, off)
        slot = plane_slot(shard, source, *cuts[way])
        return pltpu.make_async_remote_copy(
            slot, slot, wqs.at[way, (off - 1) * max(sizes) + onward - 1], wpr.at[shard, source],
            **to("rep", beside_me(1 - way, onward)))

    def weight_from(shard, source):
        slot = plane_slot(shard, source)
        return pltpu.make_async_remote_copy(
            slot, slot, wps.at[0, 0], wpr.at[shard, source], **to("rep", source))

    def plane_sent(sem, count):
        return pltpu.make_async_remote_copy(
            plane_bytes(count), plane_bytes(count), sem, wpr.at[0, 0], **to("rep", me))

    def half_copy(off):
        return pltpu.make_async_remote_copy(
            halves.at[t], halves.at[t], hs.at[off - 1], hr.at[off - 1], **to("tp", lax.rem(t + off, ntp)))

    def edge_half_copy(off):
        other = lax.rem(t + off, ntp)
        return pltpu.make_async_remote_copy(
            edge_half.at[pl.ds(pl.multiple_of(other * band, band), band), :], edge_got.at[t],
            gs.at[off - 1], gr.at[off - 1], **to("tp", other))

    def out_copy(target):
        return pltpu.make_async_remote_copy(edge_out, edge_in.at[t], os.at[0], orr.at[0], **to("fsdp", target))

    def out_relay(off):
        return pltpu.make_async_remote_copy(
            edge_in.at[t], edge_in.at[t], qs.at[off - 1], qr.at[off - 1], **to("tp", lax.rem(t + off, ntp)))

    def grad_out(p):
        return pltpu.make_async_copy(grad_v.at[p], grad.at[:, cols(p)], ds.at[0])

    def upd_out(p):
        return pltpu.make_async_copy(upd_v.at[p], upd.at[:, cols(p)], us.at[0])

    proj_out = pltpu.make_async_copy(proj_v, proj, loc.at[4])

    def group(stage, i):
        turn = lax.rem(i, 2) if low == high else 0
        along = turn if stage == 0 else 1 - turn
        size = sizes[stage]
        at = (1 - along) * mine + along * rest

        def peer(off):
            pos = lax.rem(at + off, size)
            return (1 - along) * (rest * low + pos) + along * (pos * low + mine)

        return size, at, peer

    def vote_copy(stage, i, off):
        _, at, peer = group(stage, i)
        slot = (ones, pairs)[stage].at[i, at]
        send, recv = ((vs, vr), (ts, tr))[stage]
        return pltpu.make_async_remote_copy(slot, slot, send.at[off - 1], recv.at[i, off - 1], **to("rep", peer(off)))

    def turned(source, target):
        for b in range(ntp):
            target[b * tp_cols:(b + 1) * tp_cols, :] = source[b].T

    def weight_step(s):
        for h in range(1, n - 1):
            for send, recv, shard, target, edge in (
                (wrs, wrr, z - h, z + 1, z - h == 0), (wls, wlr, z + h, z - 1, z + h == n - 1)):
                at = WLAG * (h - 1) + jnp.where(edge, BURST, 0)
                on = (target > 0) & (target < n - 1)
                here = inner & (shard >= 0) & (shard < n)

                @pl.when(here & (s == at))
                def _():
                    @pl.loop(0, chunks)
                    def _(c):
                        weight_line(False, shard, c, send, recv, z).wait_recv()

                        @pl.when(on)
                        def _():
                            weight_line(False, shard, c, send, recv, target).start()

                    for way in range(2):
                        for off in range(1, sizes[way]):
                            weight_plane(shard, way, off).start()

                @pl.when(here & (s == at + RELAY))
                def _():
                    for way in range(2):
                        for off in range(1, sizes[way]):
                            weight_from(shard, before_me(way, off)).wait_recv()
                            if cuts[way][0] < cuts[way][1]:
                                for onward in range(1, sizes[1 - way]):
                                    weight_relay(shard, way, off, onward).start()

    def weights_ready(shard):
        for a in range(1, low):
            for b in range(1, high):
                source = lax.rem(rest + high - b, high) * low + lax.rem(mine + low - a, low)
                weight_from(shard, source).wait_recv()

    def weights_sent():
        for way in range(2):
            for off in range(1, sizes[way]):
                plane_sent(wps.at[way, off - 1], chunks).wait_send()
                if cuts[way][0] < cuts[way][1]:
                    for onward in range(1, sizes[1 - way]):
                        plane_sent(wqs.at[way, (off - 1) * max(sizes) + onward - 1],
                                   cuts[way][1] - cuts[way][0]).wait_send()

    def token_step(s):
        @pl.when(beside & (s < pieces))
        def _():
            @pl.when(s == 0)
            def _():
                edge_cot(z).wait_recv()
                for off in range(1, ntp):
                    edge_cot_relay(off).start()
                for off in range(1, ntp):
                    edge_cot_relay(off).wait_recv()
                turned(edge_cots, edge_cots_t)

            edge_tok(s, z).wait_recv()
            total = jnp.dot(edge_cots_t[...], edge_toks[s], preferred_element_type=F32) + part[s].astype(F32)

            @pl.when(z == 1)
            def _():
                right_buf[s] = total.astype(BF16)

            @pl.when(z == n - 2)
            def _():
                left_buf[s] = total.astype(BF16)

    def sum_step(s):
        for first in (True, False):
            for j in range(n - 2, 0, -1):
                for flow in flows:
                    buf, _, _, way, depth = flow
                    p = s - LAG * (depth - 1) - HOLD * (n - 1 - depth - j)
                    k = z + way * j
                    ok = (p >= 0) & (p < pieces) & (k >= 0) & (k < n)

                    @pl.when(ok & ((depth == 1) if first else (depth > 1)))
                    def _():
                        if not first:
                            rk = pl.ds(pl.multiple_of(k * rows, rows), rows)
                            sum_copy(flow, p, k, False).wait_recv()
                            buf[p, rk, :] = (buf[p, rk, :].astype(F32) + part[p, rk, :].astype(F32)).astype(BF16)
                        sum_copy(flow, p, k).start()

    def vote(p):
        for flow in flows:
            @pl.when(flow[4] > 1)
            def _():
                sum_copy(flow, p, z, False).wait_recv()
        keep = jnp.where(beside, 0.0, 1.0).astype(F32)
        for q in range(split):
            i = p * split + q
            cut = slice(q * part_width, (q + 1) * part_width)
            at = pl.ds(pl.multiple_of(i * part_width, LANES), part_width)
            g = (part[p, own_rows, cut].astype(F32) * keep + right_buf[p, own_rows, cut].astype(F32)
                 + left_buf[p, own_rows, cut].astype(F32)) * scale
            grad_v[p, :, cut] = g.astype(BF16)
            blended = BETA_ONE * mom_v[:, at].astype(F32) + (1.0 - BETA_ONE) * g
            size, place, _ = group(0, i)
            ones[i, place] = jnp.clip(blended / SOFT_WIDTH, -1.0, 1.0).astype(BF16)
            for off in range(1, size):
                vote_copy(0, i, off).start()
        grad_out(p).start()

    def added(stage, i):
        size, place, _ = group(stage, i)
        for off in range(1, size):
            vote_copy(stage, i, off).wait_recv()
        buf = (ones, pairs)[stage]
        total = buf[i, 0].astype(F32)
        for b in range(1, size):
            total = total + buf[i, b].astype(F32)
        return total

    def count(p):
        for q in range(split):
            i = p * split + q
            total = added(0, i)
            size, place, _ = group(1, i)
            pairs[i, place] = total.astype(BF16)
            for off in range(1, size):
                vote_copy(1, i, off).start()

    def finish(p):
        for q in range(split):
            upd_v[p, :, q * part_width:(q + 1) * part_width] = jnp.clip(
                added(1, p * split + q), -1.0, 1.0).astype(BF16)
        upd_out(p).start()

    first_proj = max(BURST + WLAG * (n - 3), WLAG * (n - 2)) + RELAY + 2
    per = -(-pieces // PROJ_STEPS)
    speed = 3
    first_edge = min(first_proj, pieces - -(-pieces // speed))

    def product(p, toks):
        return lax.dot_general(
            toks, weights[:, cols(p)], (((1,), (1,)), ((), ())), preferred_element_type=F32)

    def project(s):
        @pl.when(inner & (s == first_edge))
        def _():
            for shard in range(n):
                @pl.when(shard != z)
                def _():
                    weights_ready(shard)
            halves[t] = jnp.zeros(halves.shape[1:], F32)
            edge_half[...] = jnp.zeros(edge_half.shape, F32)

        @pl.when(beside & (s >= first_edge) & (s < pieces))
        def _():
            @pl.loop(jnp.minimum(s, speed * (s - first_edge)), jnp.minimum(s + 1, speed * (s - first_edge + 1)))
            def _(p):
                edge_half[...] += product(p, edge_toks[p])

            @pl.when(s == pieces - 1)
            def _():
                for off in range(1, ntp):
                    edge_half_copy(off).start()

        @pl.when(beside & (s == pieces))
        def _():
            total = edge_half[pl.ds(pl.multiple_of(t * band, band), band), :]
            for off in range(1, ntp):
                edge_half_copy(off).wait_recv()
            for off in range(1, ntp):
                total = total + edge_got[lax.rem(t + off, ntp)]
            edge_out[...] = total.astype(BF16)

            @pl.when(z == 1)
            def _():
                out_copy(z - 1).start()

            @pl.when(z == n - 2)
            def _():
                out_copy(z + 1).start()

        @pl.when(inner & (s >= first_proj) & (s < first_proj + PROJ_STEPS))
        def _():
            for i in range(per):
                p = (s - first_proj) * per + i

                @pl.when(p < pieces)
                def _():
                    halves[t] += product(p, tok_v[:, cols(p)])

        @pl.when(inner & (s == first_proj + PROJ_STEPS))
        def _():
            for off in range(1, ntp):
                half_copy(off).start()

        @pl.when(inner & (s == first_proj + PROJ_STEPS + 1))
        def _():
            for off in range(1, ntp):
                half_copy(off).wait_recv()
            total = halves[0]
            for b in range(1, ntp):
                total = total + halves[b]
            proj_v[...] = total.astype(BF16)
            proj_out.start()
            for off in range(1, ntp):
                half_copy(off).wait_send()
            weights_sent()

    tok_load = pltpu.make_async_copy(tok, tok_v, loc.at[0])
    mom_load = pltpu.make_async_copy(mom.at[0], mom_v, loc.at[1])
    cot_load = pltpu.make_async_copy(cot, cots.at[t], loc.at[2])
    wgt_load = pltpu.make_async_copy(wgt, weights.at[own_rows, :], loc.at[3])
    barrier = pltpu.get_barrier_semaphore()
    for axis, at, size in (("tp", t, ntp), ("rep", me, nrep)):
        for off in range(1, size):
            pl.semaphore_signal(barrier, inc=1, **to(axis, lax.rem(at + off, size)))

    @pl.when(z > 0)
    def _():
        pl.semaphore_signal(barrier, inc=1, **to("fsdp", z - 1))

    @pl.when(z < n - 1)
    def _():
        pl.semaphore_signal(barrier, inc=1, **to("fsdp", z + 1))

    cot_load.start()
    tok_load.start()
    wgt_load.start()
    mom_load.start()
    pl.semaphore_wait(barrier, ntp + nrep - 2 + jnp.where(inner, 2, 1))

    for edge, target, send, recv in ((0, z + 1, wrs, wrr), (n - 1, z - 1, wls, wlr)):
        @pl.when(z == edge)
        def _():
            edge_cot(target).start()
            for p in range(BURST):
                edge_tok(p, target).start()

    for off in range(1, ntp):
        cot_copy(off).start()

    for send, recv, target in ((wrs, wrr, z + 1), (wls, wlr, z - 1)):
        @pl.when(inner & (target > 0) & (target < n - 1))
        def _():
            @pl.loop(0, chunks)
            def _(c):
                weight_line(True, z, c, send, recv, target).start()

    for edge, target, send, recv in ((0, z + 1, wrs, wrr), (n - 1, z - 1, wls, wlr)):
        @pl.when(z == edge)
        def _():
            @pl.loop(0, chunks)
            def _(c):
                weight_line(True, z, c, send, recv, target).start()

            @pl.loop(BURST, pieces)
            def _(p):
                edge_tok(p, target).start()

    for buf, edge in ((right_buf, 0), (left_buf, n - 1)):
        @pl.when(z == edge)
        def _():
            buf[:, edge * rows:(edge + 1) * rows, :] = jnp.zeros((pieces, rows, width), BF16)
    cot_load.wait()
    for off in range(1, ntp):
        cot_copy(off).wait_recv()
    turned(cots, cots_t)
    tok_load.wait()

    @pl.loop(0, pieces)
    def _(p):
        part[p] = jnp.dot(cots_t[...], tok_v[:, cols(p)], preferred_element_type=F32).astype(BF16)

    wgt_load.wait()
    mom_load.wait()

    deep = jnp.maximum(z, n - 1 - z)
    voting = LAG * (deep - 1) + HOLD * (n - 1 - deep)
    last = max(pieces + LAG * (n - 2), first_proj + PROJ_STEPS + 2)

    @pl.loop(0, last)
    def _(s):
        weight_step(s)
        token_step(s)
        sum_step(s)
        for work, at in ((vote, voting), (count, voting + COUNT), (finish, voting + COUNT + FINISH)):
            @pl.when((s >= at) & (s < at + pieces))
            def _():
                work(s - at)
        project(s)

    @pl.loop(jnp.minimum(last - voting - COUNT, pieces), pieces)
    def _(p):
        count(p)

    for edge, target, send, recv in ((0, z + 1, wrs, wrr), (n - 1, z - 1, wls, wlr)):
        @pl.when(z == edge)
        def _():
            out_copy(target).wait_recv()
            for off in range(1, ntp):
                out_relay(off).start()
            edge_cot(target).wait_send()

            line_sent(z, send).wait_send()
            whole = pltpu.make_async_remote_copy(tok_v, tok_v, ks.at[0], kr.at[0], **to("fsdp", z))
            whole.wait_send()
            for off in range(1, ntp):
                out_relay(off).wait_recv()
            for b in range(ntp):
                proj_v[b * band:(b + 1) * band, :] = edge_in[b]
            proj_out.start()
            for off in range(1, ntp):
                out_relay(off).wait_send()

    @pl.loop(jnp.minimum(last - voting - COUNT - FINISH, pieces), pieces)
    def _(p):
        finish(p)

    for off in range(1, ntp):
        cot_copy(off).wait_send()

    @pl.when(beside)
    def _():
        for off in range(1, ntp):
            edge_cot_relay(off).wait_send()
            edge_half_copy(off).wait_send()
        out_copy(z).wait_send()

    for shard in range(n):
        for send, recv, target, ok in ((wrs, wrr, z + 1, shard <= z), (wls, wlr, z - 1, shard >= z)):
            @pl.when(inner & ok & (target > 0) & (target < n - 1))
            def _():
                line_sent(shard, send).wait_send()

    for flow in flows:
        _, _, _, way, depth = flow
        for k in range(n):
            @pl.when((depth > 0) & ((k - z) * way > 0))
            def _():
                sums_sent(flow, k).wait_send()

    for stage in range(2):
        buf, send, recv = ((ones, vs, vr), (pairs, ts, tr))[stage]
        for off in range(1, max(sizes)):
            if off < sizes[stage]:
                pltpu.make_async_remote_copy(
                    buf.at[:, 0], buf.at[:, 0], send.at[off - 1], recv.at[0, 0], **to("rep", me)).wait_send()
    pltpu.make_async_copy(grad_v, grad_v, ds.at[0]).wait()
    pltpu.make_async_copy(upd_v, upd_v, us.at[0]).wait()

    proj_out.wait()


def shards(n, nrep, ntp, tokens, cotangent, weight, momentum):
    held, half = tokens.shape
    rows, cols = weight.shape[0], weight.shape[0] * n
    width = min(WIDTH, half)
    pieces = half // width
    low = max(r for r in range(1, nrep + 1) if nrep % r == 0 and r * r <= nrep)
    chunks = max(1, min(4, half // (nrep * LANES)))
    most = max(low, nrep // low)
    scale = 1.0 / math.sqrt(held * n)
    dma = pltpu.SemaphoreType.DMA
    split = 2 if width % (2 * LANES) == 0 else 1
    hbm = pl.BlockSpec(memory_space=pltpu.HBM)
    place = pl.BlockSpec(memory_space=pl.ANY)
    given = [pltpu.with_memory_space_constraint(a, pltpu.HBM) for a in (tokens, cotangent, weight, momentum)]
    projected, update, gradient = pl.pallas_call(
        functools.partial(step, (n, nrep, ntp, pieces, width, rows, low, chunks), scale),
        out_shape=(
            jax.ShapeDtypeStruct((held, cols), BF16),
            jax.ShapeDtypeStruct((rows, half), BF16),
            jax.ShapeDtypeStruct((rows, half), BF16),
        ),
        in_specs=[hbm] * 4,
        out_specs=(place,) * 3,
        scratch_shapes=[
            pltpu.VMEM((held, half), BF16),
            pltpu.VMEM((rows, half), BF16),
            pltpu.VMEM((pieces, cols, width), BF16),
            pltpu.VMEM((pieces, cols, width), BF16),
            pltpu.VMEM((pieces, cols, width), BF16),
            pltpu.VMEM((cols, half), BF16),
            pltpu.VMEM((ntp,) + cotangent.shape, BF16),
            pltpu.VMEM((ntp,) + cotangent.shape, BF16),
            pltpu.VMEM((cols, held), BF16),
            pltpu.VMEM((cols, held), BF16),
            pltpu.VMEM((pieces, held, width), BF16),
            pltpu.VMEM((ntp, held, cols), F32),
            pltpu.VMEM((held, cols), F32),
            pltpu.VMEM((ntp, held // ntp, cols), F32),
            pltpu.VMEM((held // ntp, cols), BF16),
            pltpu.VMEM((ntp, held // ntp, cols), BF16),
            pltpu.VMEM((held, cols), BF16),
            pltpu.VMEM((pieces, rows, width), BF16),
            pltpu.VMEM((pieces, rows, width), BF16),
            pltpu.VMEM((pieces * split, most, rows, width // split), BF16),
            pltpu.VMEM((pieces * split, most, rows, width // split), BF16),
        ]
        + [dma((5,))]
        + [dma((max(1, ntp - 1),))] * 2
        + [dma((1,))] * 2
        + [dma((max(1, ntp - 1),))] * 2
        + [dma((1,)), dma((pieces,))]
        + [dma((n,)), dma((pieces, n - 2))] * 2
        + [dma((n,)), dma((n, chunks))] * 2
        + [dma((2, max(1, most - 1))), dma((n, nrep)), dma((2, most * most))]
        + [dma((max(1, ntp - 1),))] * 4
        + [dma((1,))] * 2
        + [dma((max(1, ntp - 1),))] * 2
        + [dma((max(1, most - 1),)), dma((pieces * split, max(1, most - 1)))] * 2
        + [dma((1,))] * 2,
        compiler_params=pltpu.CompilerParams(
            collective_id=0, has_side_effects=True, vmem_limit_bytes=44 * 1024 * 1024
        ),
    )(*given)
    renewed = BETA_TWO * momentum.astype(F32) + (1.0 - BETA_TWO) * gradient.astype(F32)[None]
    return (projected, update.astype(F32), renewed)


def solution(mesh):
    sizes = dict(mesh.shape)
    return jax.shard_map(
        functools.partial(shards, sizes["fsdp"], sizes["rep"], sizes["tp"]),
        mesh=mesh,
        in_specs=(
            P(("rep", "fsdp"), "tp"),
            P(("rep", "fsdp"), "tp"),
            P("fsdp", "tp"),
            P("rep", "fsdp", "tp"),
        ),
        out_specs=(P(("rep", "fsdp"), None), P("fsdp", "tp"), P("rep", "fsdp", "tp")),
        check_vma=False,
    )
```

time: 95.6 us -> 83.5 us (0.87)
  Pallas kernels: 85.9 us -> 78.8 us
  local copies, waits for them, and re-layouts: 5.64 us -> 0.71 us
    pallas_call x1, Pallas kernels: 85.9 us -> 78.8 us  [shards(): pl.pallas_call(functools.partial(step, (n, nrep, ntp, pieces, width, rows...]
    unnamed x9 -> x3, local copies, waits for them, and re-layouts: 5.64 us -> 0.71 us
where the time goes in v2:
time: 83.5 us; the launch traced here: 83.3 us
  Pallas kernels  78.8 us (94%)
  other arithmetic  3.19 us (4%)
    pallas_call x1, Pallas kernels, shards(): pl.pallas_call(functools.partial(step, (n, nrep, ntp, pieces, width, rows...  78.8 us

profile of v2, /device:TPU:0, one launch (start us, length us, event | category | flops | bytes accessed | tf_op | source)
XLA Modules:
  0.0 83.3 jit_solution(4357844116982295936)
XLA Ops:
  0.6 78.8 %shard_map.67 = (bf16[256,512]{1,0:T(8,128)(2,1)S(1)}, bf16[128,4096]{1,0:T(8,128)(2,1)S(1)}, bf16[128,4096]{1,0:T(8,128)(2,1)S(1)}) custom-call(bf16[256,4096]{1,0:T(8,128)(2,1)} %tok.1, bf16[256,256]{1,0:T(8,128)(2,1)} %cot.1, bf16[128,4096]{1,0:T(8,128)(2,1)} %wgt.1, bf16[1,128,4096]{2,1,0:T(8,128)(2,1)} %mom.1), custom_call_target="tpu_custom_call" | custom-call | tf_op jit(solution)/shard_map/pallas_call | solution.py:554
  79.4 0.0 copy-start
  79.4 1.5 %convert_element_type.9 = f32[128,4096]{1,0:T(8,128)} convert(bf16[128,4096]{1,0:T(8,128)(2,1)S(1)} %get-tuple-element.7) | non-fusion elementwise | flops 524288 | bytes 3145728 | tf_op jit(solution)/shard_map/convert_element_type | solution.py:604
  81.0 0.0 copy-done
  81.0 1.7 %bitcast_add_fusion = f32[1,128,4096]{2,1,0:T(8,128)} fusion(bf16[128,4096]{1,0:T(8,128)(2,1)S(1)} %get-tuple-element.8, bf16[1,128,4096]{2,1,0:T(8,128)(2,1)S(1)} %copy-done), kind=kLoop, calls=%fused_computation | loop fusion | flops 2621440 | bytes 4194304 | tf_op jit(solution)/shard_map/add | solution.py:603
  82.6 0.7 copy.8
Async XLA Ops:
  79.4 1.5 %copy-start = (bf16[1,128,4096]{2,1,0:T(8,128)(2,1)S(1)}, bf16[1,128,4096]{2,1,0:T(8,128)(2,1)}, u32[]{:S(2)}) copy-start(bf16[1,128,4096]{2,1,0:T(8,128)(2,1)} %mom.1) | copy-start | bytes 3145732

commit v3 on v2

--- a/solution.py
+++ b/solution.py
@@ -14,7 +14,7 @@
 LANES = 128
 WIDTH = 256
 LAG = 3
-HOLD = 1
+HOLD = 0
 BURST = 2
 WLAG = 2
 RELAY = 3
@@ -50,7 +50,8 @@
     def cols(p):
         return pl.ds(pl.multiple_of(p * width, LANES), width)
 
-    flows = ((right_buf, rs_s, rs_r, 1, z), (left_buf, ls_s, ls_r, -1, n - 1 - z))
+    got = rs_r if n < 5 else ls_r
+    flows = ((right_buf, rs_s, rs_r, 1, z), (left_buf, ls_s, got, -1, n - 1 - z))
 
     def cot_copy(off):
         return pltpu.make_async_remote_copy(
@@ -357,6 +358,8 @@
                 total = total + edge_got[lax.rem(t + off, ntp)]
             edge_out[...] = total.astype(BF16)
 
+        @pl.when(beside & (s == pieces - 1 + LAG * (n - 3)))
+        def _():
             @pl.when(z == 1)
             def _():
                 out_copy(z - 1).start()
@@ -588,7 +591,8 @@
         + [dma((1,))] * 2
         + [dma((max(1, ntp - 1),))] * 2
         + [dma((1,)), dma((pieces,))]
-        + [dma((n,)), dma((pieces, n - 2))] * 2
+        + [dma((n,)), dma((pieces, n - 2))]
+        + [dma((n,)), dma((pieces, n - 2) if n > 4 else (1,))]
         + [dma((n,)), dma((n, chunks))] * 2
         + [dma((2, max(1, most - 1))), dma((n, nrep)), dma((2, most * most))]
         + [dma((max(1, ntp - 1),))] * 4

time: 83.5 us -> 81.4 us (0.975)
  Pallas kernels: 78.8 us -> 76.7 us
    pallas_call x1, Pallas kernels: 78.8 us -> 76.7 us  [shards(): pl.pallas_call(functools.partial(step, (n, nrep, ntp, pieces, width, rows...]
where the time goes in v3:
time: 81.4 us; the launch traced here: 81.3 us
  Pallas kernels  76.7 us (94%)
  other arithmetic  3.19 us (4%)
    pallas_call x1, Pallas kernels, shards(): pl.pallas_call(functools.partial(step, (n, nrep, ntp, pieces, width, rows...  76.7 us
    add x1, other arithmetic, shards(): BETA_TWO * momentum.astype(F32)  1.66 us

profile of v3, /device:TPU:0, one launch (start us, length us, event | category | flops | bytes accessed | tf_op | source)
XLA Modules:
  0.0 81.3 jit_solution(16302649770996638136)
XLA Ops:
  0.6 76.7 %shard_map.67 = (bf16[256,512]{1,0:T(8,128)(2,1)S(1)}, bf16[128,4096]{1,0:T(8,128)(2,1)S(1)}, bf16[128,4096]{1,0:T(8,128)(2,1)S(1)}) custom-call(bf16[256,4096]{1,0:T(8,128)(2,1)} %tok.1, bf16[256,256]{1,0:T(8,128)(2,1)} %cot.1, bf16[128,4096]{1,0:T(8,128)(2,1)} %wgt.1, bf16[1,128,4096]{2,1,0:T(8,128)(2,1)} %mom.1), custom_call_target="tpu_custom_call" | custom-call | tf_op jit(solution)/shard_map/pallas_call | solution.py:557
  77.3 0.0 copy-start
  77.4 1.5 %convert_element_type.9 = f32[128,4096]{1,0:T(8,128)} convert(bf16[128,4096]{1,0:T(8,128)(2,1)S(1)} %get-tuple-element.7) | non-fusion elementwise | flops 524288 | bytes 3145728 | tf_op jit(solution)/shard_map/convert_element_type | solution.py:608
  78.9 0.0 copy-done
  78.9 1.7 %bitcast_add_fusion = f32[1,128,4096]{2,1,0:T(8,128)} fusion(bf16[128,4096]{1,0:T(8,128)(2,1)S(1)} %get-tuple-element.8, bf16[1,128,4096]{2,1,0:T(8,128)(2,1)S(1)} %copy-done), kind=kLoop, calls=%fused_computation | loop fusion | flops 2621440 | bytes 4194304 | tf_op jit(solution)/shard_map/add | solution.py:607
  80.5 0.7 copy.8
Async XLA Ops:
  77.3 1.5 %copy-start = (bf16[1,128,4096]{2,1,0:T(8,128)(2,1)S(1)}, bf16[1,128,4096]{2,1,0:T(8,128)(2,1)}, u32[]{:S(2)}) copy-start(bf16[1,128,4096]{2,1,0:T(8,128)(2,1)} %mom.1) | copy-start | bytes 3145732

commit v4 on v3

--- a/solution.py
+++ b/solution.py
@@ -26,10 +26,10 @@
 BF16 = jnp.bfloat16
 
 
-def step(dims, scale, tok, cot, wgt, mom, proj, upd, grad, *scratch):
+def step(dims, scale, tok, cot, wgt, mom, proj, upd, new, *scratch):
     (n, nrep, ntp, pieces, width, rows, low, chunks) = dims
     (tok_v, mom_v, part, right_buf, left_buf, weights, cots, edge_cots, cots_t, edge_cots_t, edge_toks,
-     halves, edge_half, edge_got, edge_out, edge_in, proj_v, upd_v, grad_v, ones, pairs) = scratch[:21]
+     halves, edge_half, edge_got, edge_out, edge_in, proj_v, upd_v, new_v, ones, pairs) = scratch[:21]
     (loc, cs, cr, es, er, fs, fr, ks, kr, rs_s, rs_r, ls_s, ls_r, wrs, wrr, wls, wlr, wps, wpr, wqs,
      hs, hr, gs, gr, os, orr, qs, qr, vs, vr, ts, tr, us, ds) = scratch[21:]
     held_rows = tok.shape[0]
@@ -158,8 +158,8 @@
         return pltpu.make_async_remote_copy(
             edge_in.at[t], edge_in.at[t], qs.at[off - 1], qr.at[off - 1], **to("tp", lax.rem(t + off, ntp)))
 
-    def grad_out(p):
-        return pltpu.make_async_copy(grad_v.at[p], grad.at[:, cols(p)], ds.at[0])
+    def new_out(p):
+        return pltpu.make_async_copy(new_v.at[p], new.at[:, cols(p)], ds.at[0])
 
     def upd_out(p):
         return pltpu.make_async_copy(upd_v.at[p], upd.at[:, cols(p)], us.at[0])
@@ -286,13 +286,14 @@
             at = pl.ds(pl.multiple_of(i * part_width, LANES), part_width)
             g = (part[p, own_rows, cut].astype(F32) * keep + right_buf[p, own_rows, cut].astype(F32)
                  + left_buf[p, own_rows, cut].astype(F32)) * scale
-            grad_v[p, :, cut] = g.astype(BF16)
-            blended = BETA_ONE * mom_v[:, at].astype(F32) + (1.0 - BETA_ONE) * g
+            held = mom_v[:, at].astype(F32)
+            new_v[p, :, cut] = BETA_TWO * held + (1.0 - BETA_TWO) * g
+            blended = BETA_ONE * held + (1.0 - BETA_ONE) * g
             size, place, _ = group(0, i)
             ones[i, place] = jnp.clip(blended / SOFT_WIDTH, -1.0, 1.0).astype(BF16)
             for off in range(1, size):
                 vote_copy(0, i, off).start()
-        grad_out(p).start()
+        new_out(p).start()
 
     def added(stage, i):
         size, place, _ = group(stage, i)
@@ -316,7 +317,7 @@
     def finish(p):
         for q in range(split):
             upd_v[p, :, q * part_width:(q + 1) * part_width] = jnp.clip(
-                added(1, p * split + q), -1.0, 1.0).astype(BF16)
+                added(1, p * split + q), -1.0, 1.0)
         upd_out(p).start()
 
     first_proj = max(BURST + WLAG * (n - 3), WLAG * (n - 2)) + RELAY + 2
@@ -534,10 +535,19 @@
             if off < sizes[stage]:
                 pltpu.make_async_remote_copy(
                     buf.at[:, 0], buf.at[:, 0], send.at[off - 1], recv.at[0, 0], **to("rep", me)).wait_send()
-    pltpu.make_async_copy(grad_v, grad_v, ds.at[0]).wait()
+    pltpu.make_async_copy(new_v, new_v, ds.at[0]).wait()
     pltpu.make_async_copy(upd_v, upd_v, us.at[0]).wait()
 
     proj_out.wait()
+
+
+def settle(proj, upd, new, proj_to, upd_to, mom_to, sems):
+    copies = [pltpu.make_async_copy(source, target, sems.at[i]) for i, (source, target) in enumerate(
+        ((upd, upd_to), (new, mom_to.at[0]), (proj, proj_to)))]
+    for copy in copies:
+        copy.start()
+    for copy in copies:
+        copy.wait()
 
 
 def shards(n, nrep, ntp, tokens, cotangent, weight, momentum):
@@ -554,12 +564,12 @@
     hbm = pl.BlockSpec(memory_space=pltpu.HBM)
     place = pl.BlockSpec(memory_space=pl.ANY)
     given = [pltpu.with_memory_space_constraint(a, pltpu.HBM) for a in (tokens, cotangent, weight, momentum)]
-    projected, update, gradient = pl.pallas_call(
+    projected, update, renewed = pl.pallas_call(
         functools.partial(step, (n, nrep, ntp, pieces, width, rows, low, chunks), scale),
         out_shape=(
             jax.ShapeDtypeStruct((held, cols), BF16),
-            jax.ShapeDtypeStruct((rows, half), BF16),
-            jax.ShapeDtypeStruct((rows, half), BF16),
+            jax.ShapeDtypeStruct((rows, half), F32),
+            jax.ShapeDtypeStruct((rows, half), F32),
         ),
         in_specs=[hbm] * 4,
         out_specs=(place,) * 3,
@@ -581,8 +591,8 @@
             pltpu.VMEM((held // ntp, cols), BF16),
             pltpu.VMEM((ntp, held // ntp, cols), BF16),
             pltpu.VMEM((held, cols), BF16),
-            pltpu.VMEM((pieces, rows, width), BF16),
-            pltpu.VMEM((pieces, rows, width), BF16),
+            pltpu.VMEM((pieces, rows, width), F32),
+            pltpu.VMEM((pieces, rows, width), F32),
             pltpu.VMEM((pieces * split, most, rows, width // split), BF16),
             pltpu.VMEM((pieces * split, most, rows, width // split), BF16),
         ]
@@ -604,8 +614,18 @@
             collective_id=0, has_side_effects=True, vmem_limit_bytes=44 * 1024 * 1024
         ),
     )(*given)
-    renewed = BETA_TWO * momentum.astype(F32) + (1.0 - BETA_TWO) * gradient.astype(F32)[None]
-    return (projected, update.astype(F32), renewed)
+    return pl.pallas_call(
+        settle,
+        out_shape=(
+            jax.ShapeDtypeStruct((held, cols), BF16),
+            jax.ShapeDtypeStruct((rows, half), F32),
+            jax.ShapeDtypeStruct((1, rows, half), F32),
+        ),
+        in_specs=[place] * 3,
+        out_specs=(hbm,) * 3,
+        scratch_shapes=[dma((3,))],
+        compiler_params=pltpu.CompilerParams(vmem_limit_bytes=4 * 1024 * 1024),
+    )(projected, update, renewed)
 
 
 def solution(mesh):

time: 81.4 us -> 79.6 us (0.978)
  other arithmetic: 3.19 us -> 0 us
  Pallas kernels: 76.7 us -> 78.8 us
    pallas_call x0 -> x1, Pallas kernels: none -> 2.11 us  [shards(): pl.pallas_call(settle, out_shape=(jax.ShapeDtypeStruct((held, cols), BF16...]
    add x1 -> x0, other arithmetic: 1.66 us -> none  [shards(): BETA_TWO * momentum.astype(F32)]
    convert_element_type x1 -> x0, other arithmetic: 1.53 us -> none  [shards(): return (projected, update.astype(F32), renewed)]
where the time goes in v4:
time: 79.6 us; the launch traced here: 79.5 us
  Pallas kernels  78.8 us (99%)
    pallas_call x1, Pallas kernels, shards(): pl.pallas_call(functools.partial(step, (n, nrep, ntp, pieces, width, rows...  76.7 us
    pallas_call x1, Pallas kernels, shards(): pl.pallas_call(settle, out_shape=(jax.ShapeDtypeStruct((held, cols), BF16...  2.11 us

profile of v4, /device:TPU:0, one launch (start us, length us, event | category | flops | bytes accessed | tf_op | source)
XLA Modules:
  0.0 79.5 jit_solution(5745452687230667961)
XLA Ops:
  0.6 76.7 %shard_map.67 = (bf16[256,512]{1,0:T(8,128)(2,1)S(1)}, f32[128,4096]{1,0:T(8,128)S(1)}, f32[128,4096]{1,0:T(8,128)S(1)}) custom-call(bf16[256,4096]{1,0:T(8,128)(2,1)} %tok.1, bf16[256,256]{1,0:T(8,128)(2,1)} %cot.1, bf16[128,4096]{1,0:T(8,128)(2,1)} %wgt.1, bf16[1,128,4096]{2,1,0:T(8,128)(2,1)} %mom.1), custom_call_target="tpu_custom_call" | custom-call | tf_op jit(solution)/shard_map/pallas_call | solution.py:567
  77.4 2.1 %shard_map.68 = (bf16[256,512]{1,0:T(8,128)(2,1)}, f32[128,4096]{1,0:T(8,128)}, f32[1,128,4096]{2,1,0:T(8,128)}) custom-call(bf16[256,512]{1,0:T(8,128)(2,1)S(1)} %get-tuple-element.6.proj, f32[128,4096]{1,0:T(8,128)S(1)} %get-tuple-element.7.upd, f32[128,4096]{1,0:T(8,128)S(1)} %get-tuple-element.8.new), custom_call_target="tpu_custom_call" | custom-call | tf_op jit(solution)/shard_map/pallas_call | solution.py:617

commit v5 on v4

--- a/solution.py
+++ b/solution.py
@@ -21,6 +21,8 @@
 COUNT = 4
 FINISH = 4
 PROJ_STEPS = 8
+CHUNKS = 2
+STRIPS = 1
 MESH = pl.DeviceIdType.MESH
 F32 = jnp.float32
 BF16 = jnp.bfloat16
@@ -178,11 +180,19 @@
 
         return size, at, peer
 
-    def vote_copy(stage, i, off):
+    def vote_copy(stage, p, q, off):
+        i = p * split + q
         _, at, peer = group(stage, i)
         slot = (ones, pairs)[stage].at[i, at]
         send, recv = ((vs, vr), (ts, tr))[stage]
-        return pltpu.make_async_remote_copy(slot, slot, send.at[off - 1], recv.at[i, off - 1], **to("rep", peer(off)))
+        return pltpu.make_async_remote_copy(slot, slot, send.at[off - 1], recv.at[p, off - 1], **to("rep", peer(off)))
+
+    def votes_in(stage, p):
+        slots = (ones, pairs)[stage].at[pl.ds(p * split, split), 0]
+        send, recv = ((vs, vr), (ts, tr))[stage]
+        for off in range(1, sizes[stage]):
+            pltpu.make_async_remote_copy(
+                slots, slots, send.at[off - 1], recv.at[p, off - 1], **to("rep", me)).wait_recv()
 
     def turned(source, target):
         for b in range(ntp):
@@ -191,7 +201,7 @@
     def weight_step(s):
         for h in range(1, n - 1):
             for send, recv, shard, target, edge in (
-                (wrs, wrr, z - h, z + 1, z - h == 0), (wls, wlr, z + h, z - 1, z + h == n - 1)):
+                (wrs, wrr, z - h, z + 1, z - h == 0), (wls, wrr, z + h, z - 1, z + h == n - 1)):
                 at = WLAG * (h - 1) + jnp.where(edge, BURST, 0)
                 on = (target > 0) & (target < n - 1)
                 here = inner & (shard >= 0) & (shard < n)
@@ -292,13 +302,11 @@
             size, place, _ = group(0, i)
             ones[i, place] = jnp.clip(blended / SOFT_WIDTH, -1.0, 1.0).astype(BF16)
             for off in range(1, size):
-                vote_copy(0, i, off).start()
+                vote_copy(0, p, q, off).start()
         new_out(p).start()
 
     def added(stage, i):
         size, place, _ = group(stage, i)
-        for off in range(1, size):
-            vote_copy(stage, i, off).wait_recv()
         buf = (ones, pairs)[stage]
         total = buf[i, 0].astype(F32)
         for b in range(1, size):
@@ -306,15 +314,17 @@
         return total
 
     def count(p):
+        votes_in(0, p)
         for q in range(split):
             i = p * split + q
             total = added(0, i)
             size, place, _ = group(1, i)
             pairs[i, place] = total.astype(BF16)
             for off in range(1, size):
-                vote_copy(1, i, off).start()
+                vote_copy(1, p, q, off).start()
 
     def finish(p):
+        votes_in(1, p)
         for q in range(split):
             upd_v[p, :, q * part_width:(q + 1) * part_width] = jnp.clip(
                 added(1, p * split + q), -1.0, 1.0)
@@ -419,7 +429,7 @@
     mom_load.start()
     pl.semaphore_wait(barrier, ntp + nrep - 2 + jnp.where(inner, 2, 1))
 
-    for edge, target, send, recv in ((0, z + 1, wrs, wrr), (n - 1, z - 1, wls, wlr)):
+    for edge, target, send, recv in ((0, z + 1, wrs, wrr), (n - 1, z - 1, wls, wrr)):
         @pl.when(z == edge)
         def _():
             edge_cot(target).start()
@@ -429,14 +439,14 @@
     for off in range(1, ntp):
         cot_copy(off).start()
 
-    for send, recv, target in ((wrs, wrr, z + 1), (wls, wlr, z - 1)):
+    for send, recv, target in ((wrs, wrr, z + 1), (wls, wrr, z - 1)):
         @pl.when(inner & (target > 0) & (target < n - 1))
         def _():
             @pl.loop(0, chunks)
             def _(c):
                 weight_line(True, z, c, send, recv, target).start()
 
-    for edge, target, send, recv in ((0, z + 1, wrs, wrr), (n - 1, z - 1, wls, wlr)):
+    for edge, target, send, recv in ((0, z + 1, wrs, wrr), (n - 1, z - 1, wls, wrr)):
         @pl.when(z == edge)
         def _():
             @pl.loop(0, chunks)
@@ -483,7 +493,7 @@
     def _(p):
         count(p)
 
-    for edge, target, send, recv in ((0, z + 1, wrs, wrr), (n - 1, z - 1, wls, wlr)):
+    for edge, target, send, recv in ((0, z + 1, wrs, wrr), (n - 1, z - 1, wls, wrr)):
         @pl.when(z == edge)
         def _():
             out_copy(target).wait_recv()
@@ -517,7 +527,7 @@
         out_copy(z).wait_send()
 
     for shard in range(n):
-        for send, recv, target, ok in ((wrs, wrr, z + 1, shard <= z), (wls, wlr, z - 1, shard >= z)):
+        for send, recv, target, ok in ((wrs, wrr, z + 1, shard <= z), (wls, wrr, z - 1, shard >= z)):
             @pl.when(inner & ok & (target > 0) & (target < n - 1))
             def _():
                 line_sent(shard, send).wait_send()
@@ -541,13 +551,16 @@
     proj_out.wait()
 
 
-def settle(proj, upd, new, proj_to, upd_to, mom_to, sems):
-    copies = [pltpu.make_async_copy(source, target, sems.at[i]) for i, (source, target) in enumerate(
-        ((upd, upd_to), (new, mom_to.at[0]), (proj, proj_to)))]
-    for copy in copies:
-        copy.start()
-    for copy in copies:
-        copy.wait()
+def settle(strips, proj, upd, new, proj_to, upd_to, mom_to, sems):
+    size = upd.shape[1] // strips
+    pairs = ((upd, upd_to), (new, mom_to.at[0]), (proj, proj_to))
+    for b in range(strips):
+        at = pl.ds(b * size, size)
+        for i, (source, target) in enumerate(pairs[:2]):
+            pltpu.make_async_copy(source.at[:, at], target.at[:, at], sems.at[i]).start()
+    pltpu.make_async_copy(proj, proj_to, sems.at[2]).start()
+    for i, (source, target) in enumerate(pairs):
+        pltpu.make_async_copy(source, target, sems.at[i]).wait()
 
 
 def shards(n, nrep, ntp, tokens, cotangent, weight, momentum):
@@ -556,7 +569,7 @@
     width = min(WIDTH, half)
     pieces = half // width
     low = max(r for r in range(1, nrep + 1) if nrep % r == 0 and r * r <= nrep)
-    chunks = max(1, min(4, half // (nrep * LANES)))
+    chunks = max(1, min(CHUNKS, half // (nrep * LANES)))
     most = max(low, nrep // low)
     scale = 1.0 / math.sqrt(held * n)
     dma = pltpu.SemaphoreType.DMA
@@ -603,19 +616,19 @@
         + [dma((1,)), dma((pieces,))]
         + [dma((n,)), dma((pieces, n - 2))]
         + [dma((n,)), dma((pieces, n - 2) if n > 4 else (1,))]
-        + [dma((n,)), dma((n, chunks))] * 2
+        + [dma((n,)), dma((n, chunks)), dma((n,)), dma((1,))]
         + [dma((2, max(1, most - 1))), dma((n, nrep)), dma((2, most * most))]
         + [dma((max(1, ntp - 1),))] * 4
         + [dma((1,))] * 2
         + [dma((max(1, ntp - 1),))] * 2
-        + [dma((max(1, most - 1),)), dma((pieces * split, max(1, most - 1)))] * 2
+        + [dma((max(1, most - 1),)), dma((pieces, max(1, most - 1)))] * 2
         + [dma((1,))] * 2,
         compiler_params=pltpu.CompilerParams(
             collective_id=0, has_side_effects=True, vmem_limit_bytes=44 * 1024 * 1024
         ),
     )(*given)
     return pl.pallas_call(
-        settle,
+        functools.partial(settle, math.gcd(STRIPS, half // LANES)),
         out_shape=(
             jax.ShapeDtypeStruct((held, cols), BF16),
             jax.ShapeDtypeStruct((rows, half), F32),

time: 79.6 us -> 79.2 us (level)
  no operation moved by 1% of the time
where the time goes in v5:
time: 79.2 us; the launch traced here: 79 us
  Pallas kernels  78.4 us (99%)
    pallas_call x1, Pallas kernels, shards(): pl.pallas_call(functools.partial(step, (n, nrep, ntp, pieces, width, rows...  76.3 us
    pallas_call x1, Pallas kernels, shards(): pl.pallas_call(functools.partial(settle, math.gcd(STRIPS, half // LANES))...  2.11 us

profile of v5, /device:TPU:0, one launch (start us, length us, event | category | flops | bytes accessed | tf_op | source)
XLA Modules:
  0.0 79.0 jit_solution(10331628753236680316)
XLA Ops:
  0.6 76.3 %shard_map.67 = (bf16[256,512]{1,0:T(8,128)(2,1)S(1)}, f32[128,4096]{1,0:T(8,128)S(1)}, f32[128,4096]{1,0:T(8,128)S(1)}) custom-call(bf16[256,4096]{1,0:T(8,128)(2,1)} %tok.1, bf16[256,256]{1,0:T(8,128)(2,1)} %cot.1, bf16[128,4096]{1,0:T(8,128)(2,1)} %wgt.1, bf16[1,128,4096]{2,1,0:T(8,128)(2,1)} %mom.1), custom_call_target="tpu_custom_call" | custom-call | tf_op jit(solution)/shard_map/pallas_call | solution.py:580
  76.9 2.1 %shard_map.68 = (bf16[256,512]{1,0:T(8,128)(2,1)}, f32[128,4096]{1,0:T(8,128)}, f32[1,128,4096]{2,1,0:T(8,128)}) custom-call(bf16[256,512]{1,0:T(8,128)(2,1)S(1)} %get-tuple-element.6.proj, f32[128,4096]{1,0:T(8,128)S(1)} %get-tuple-element.7.upd, f32[128,4096]{1,0:T(8,128)S(1)} %get-tuple-element.8.new), custom_call_target="tpu_custom_call" | custom-call | tf_op jit(solution)/shard_map/pallas_call | solution.py:630
